TPU v7x, 256 devices: a whole 4x4x8 slice. The times are simulated.
256 devices in a mesh: dom: 8 (over y, core), feat: 32 (over z, x).
Axes of the slice: x: 4, y: 4, z: 8, core: 2. Of those that a mesh axis runs over, the one named last changes fastest.
Arguments:
- node_feats: bfloat16 [1024, 32768], P('feat', 'dom'), may hold values from -6 to 6
- send_rows: int32 [8192], P('dom'), may hold values from 0 to 4095
- hub_rows: int32 [1024], P('dom'), may hold values from 0 to 4095
- tile_dst: int32 [4096], P('dom'), may hold values from 0 to 7
- tile_src: int32 [4096], P('dom'), may hold values from 0 to 47
- tile_count: int32 [8], P('dom'), may hold values from 128 to 512, as said below
- tile_vals: bfloat16 [4096, 128, 128], P('dom'), may hold values from -0.0625 to 0.0625
- w_self: bfloat16 [1024, 1024], P('feat'), may hold values from -0.1875 to 0.1875
- w_neigh: bfloat16 [1024, 1024], P('feat'), may hold values from -0.1875 to 0.1875
- bias_vec: float32 [1024], P('feat'), may hold values from -3 to 3
- cotangent: bfloat16 [1024, 8192], P('feat', 'dom'), may hold values from -6 to 6
Outputs:
- activations: bfloat16 [1024, 8192], P('feat', 'dom')
- grad_feats: float32 [1024, 32768], P('feat', 'dom')
- grad_w_self: float32 [1024, 1024], P('feat')
- grad_w_neigh: float32 [1024, 1024], P('feat')
- grad_bias: float32 [1024], P('feat')
Inputs may be any that keep to these rules, and one draw needn't show every extreme that they name: `tile_count`: every partition has at least 128 live slots, and some partition has all 512 live; slots at or past the count are not edges: their tile_vals may hold any values and must be ignored.
All inputs are finite; a program needn't handle non-finite values.
Results may differ from a plain program's by a relative error of at most 0.0075.
Values may be sent and summed in bfloat16 or wider, within the bound.
A program may use at most 128 MiB of HBM per device.

v0:
```python
import jax
import jax.numpy as jnp
from jax import lax
from jax.sharding import PartitionSpec as P


def contract_first(left, right):
    return lax.dot_general(
        left, right, (((0,), (0,)), ((), ())), preferred_element_type=jnp.float32
    )


def contract_last(left, right):
    return lax.dot_general(
        left, right, (((1,), (1,)), ((), ())), preferred_element_type=jnp.float32
    )


def body(
    node_feats,
    send_rows,
    hub_rows,
    tile_dst,
    tile_src,
    tile_count,
    tile_vals,
    w_self,
    w_neigh,
    bias_vec,
    cotangent,
):
    feat_cols = node_feats.shape[0]
    own_rows = node_feats.shape[1]
    dst_rows = cotangent.shape[1]
    sent_total = send_rows.shape[0]
    outgoing = jnp.take(node_feats, send_rows, axis=1)
    halo_cols = lax.all_to_all(outgoing, "dom", split_axis=1, concat_axis=1, tiled=True)
    hub_cols = lax.all_gather(jnp.take(node_feats, hub_rows, axis=1), "dom", axis=1, tiled=True)
    source_table = jnp.concatenate([node_feats, halo_cols, hub_cols], axis=1)
    tile_total = source_table.shape[1] // 128
    dst_tiles = dst_rows // 128
    live_mask = (jnp.arange(tile_dst.shape[0]) < tile_count[0]).astype(jnp.float32)
    dst_hot = (tile_dst[:, None] == jnp.arange(dst_tiles)[None, :]).astype(jnp.float32) * live_mask[
        :, None
    ]
    src_hot = (tile_src[:, None] == jnp.arange(tile_total)[None, :]).astype(
        jnp.float32
    ) * live_mask[:, None]
    picked = source_table.reshape(feat_cols, tile_total, 128)[:, tile_src, :]
    products = jnp.einsum("fkj,kij->fki", picked, tile_vals, preferred_element_type=jnp.float32)
    summed = jnp.einsum("fki,ku->fui", products, dst_hot, precision=lax.Precision.HIGHEST)
    aggregate = summed.reshape(feat_cols, dst_rows).astype(jnp.bfloat16)
    dst_feats = node_feats[:, :dst_rows]
    whole_self, whole_agg = (
        lax.all_gather(dst_feats, "feat", axis=0, tiled=True),
        lax.all_gather(aggregate, "feat", axis=0, tiled=True),
    )
    pre_act = (
        jnp.dot(w_self, whole_self, preferred_element_type=jnp.float32)
        + jnp.dot(w_neigh, whole_agg, preferred_element_type=jnp.float32)
        + bias_vec[:, None]
    )
    sig_val = jax.nn.sigmoid(pre_act)
    activations = (pre_act * sig_val).astype(jnp.bfloat16)
    grad_pre = (cotangent.astype(jnp.float32) * sig_val * (1.0 + pre_act * (1.0 - sig_val))).astype(
        jnp.bfloat16
    )
    local_self = contract_last(grad_pre, whole_self)
    local_neigh = contract_last(grad_pre, whole_agg)
    local_bias = jnp.sum(grad_pre.astype(jnp.float32), axis=1)
    grad_w_self, grad_w_neigh, grad_bias = lax.psum((local_self, local_neigh, local_bias), "dom")
    both_grads = lax.psum_scatter(
        jnp.concatenate(
            [contract_first(w_self, grad_pre), contract_first(w_neigh, grad_pre)], axis=1
        ),
        "feat",
        scatter_dimension=0,
        tiled=True,
    )
    grad_self_in = both_grads[:, :dst_rows]
    grad_agg = both_grads[:, dst_rows:].astype(jnp.bfloat16)
    upstream = grad_agg.reshape(feat_cols, dst_tiles, 128)[:, tile_dst, :]
    back_terms = jnp.einsum("fki,kij->fkj", upstream, tile_vals, preferred_element_type=jnp.float32)
    placed = jnp.einsum("fkj,kt->ftj", back_terms, src_hot, precision=lax.Precision.HIGHEST)
    grad_table = placed.reshape(feat_cols, tile_total * 128)
    halo_grad = grad_table[:, own_rows : own_rows + sent_total]
    hub_grad = grad_table[:, own_rows + sent_total :]
    returned = lax.all_to_all(
        halo_grad.astype(jnp.bfloat16), "dom", split_axis=1, concat_axis=1, tiled=True
    ).astype(halo_grad.dtype)
    hub_total = lax.psum_scatter(
        hub_grad.astype(jnp.bfloat16), "dom", scatter_dimension=1, tiled=True
    ).astype(jnp.float32)
    grad_feats = grad_table[:, :own_rows]
    grad_feats = grad_feats.at[:, send_rows].add(returned)
    grad_feats = grad_feats.at[:, hub_rows].add(hub_total)
    grad_feats = grad_feats.at[:, :dst_rows].add(grad_self_in)
    return (activations, grad_feats, grad_w_self, grad_w_neigh, grad_bias)


def solution(mesh):
    return jax.shard_map(
        body,
        mesh=mesh,
        in_specs=(
            P("feat", "dom"),
            P("dom"),
            P("dom"),
            P("dom"),
            P("dom"),
            P("dom"),
            P("dom", None, None),
            P("feat", None),
            P("feat", None),
            P("feat"),
            P("feat", "dom"),
        ),
        out_specs=(P("feat", "dom"), P("feat", "dom"), P("feat", None), P("feat", None), P("feat")),
        check_vma=False,
    )
```

profile of v0, /device:TPU:2, one launch (start us, length us, event | category | flops | bytes accessed | tf_op | source)
XLA Modules:
  0.0 555.3 jit_solution(6041104265866286545)
XLA Ops:
  7.2 1.5 slice.40
  8.7 1.4 copy.77
  10.9 3.2 gather_fusion
  15.5 4.5 all-to-all-start
  22.8 13.7 %all_gather.10 = bf16[32,1024]{0,1:T(8,128)(2,1)S(1)} all-gather(bf16[32,128]{0,1:T(8,128)(2,1)S(1)} %select_bitcast_fusion), channel_id=1, replica_groups=mesh['dom'=8,'feat'=32] {'dom'}, dimensions={1}, use_global_device_ids=true | all-gather | bytes 73728 | tf_op jit(solution)/shard_map/all_gather | solution.py:38
  37.3 1.0 copy_bitcast_fusion.1
  38.4 3.5 gather_fusion.2
  41.8 13.0 %fusion.8 = f32[32,512,128]{2,0,1:T(8,128)S(1)} fusion(bf16[512,128,128]{2,1,0:T(8,128)(2,1)} %param.19, bf16[512,32,128]{2,1,0:T(8,128)(2,1)} %gather_fusion.2), kind=kOutput, calls=%fused_computation.15 | convolution fusion | flops 536870912 | bytes 29360128 | tf_op jit(solution)/shard_map/fkj,kij->fki/dot_general | solution.py:50
  54.8 8.6 %fusion.16 = bf16[8,32,128]{2,0,1:T(8,128)(2,1)S(1)} fusion(f32[32,512,128]{2,0,1:T(8,128)S(1)} %fusion.8, f32[512]{0:T(512)S(1)} %fusion.30, s32[512]{0:T(512)S(1)} %copy-done.6), kind=kOutput, calls=%fused_computation.22 | convolution fusion | flops 201367552 | bytes 8458240 | tf_op jit(solution)/shard_map/fki,ku->fui/dot_general | solution.py:51
  64.3 26.6 %all-gather.3.cloned.1.call-done = bf16[1024,1024]{1,0:T(8,128)(2,1)} async-done(((bf16[32,1024]{1,0:T(8,128)(2,1)}), bf16[1024,1024]{1,0:T(8,128)(2,1)}) %all-gather.3.cloned.1.call-update) | async-done | bytes 2097168 | tf_op jit(solution)/shard_map/all_gather | solution.py:55
  90.9 2.1 fusion.35
  93.0 76.2 %all-gather.5.cloned.1.call-done = bf16[1024,1024]{1,0:T(8,128)(2,1)} async-done(((bf16[32,1024]{1,0:T(8,128)(2,1)}), bf16[1024,1024]{1,0:T(8,128)(2,1)}) %all-gather.5.cloned.1.call-update) | async-done | bytes 2097168 | tf_op jit(solution)/shard_map/all_gather | solution.py:56
  169.2 2.8 convert_reduce_fusion
  173.5 4.1 pad_maximum_fusion
  177.6 9.2 %copy.95 = f32[1024,2048]{1,0:T(8,128)} copy(f32[1024,2048]{0,1:T(8,128)} %pad_maximum_fusion) | data formatting | bytes 16777216
  187.5 0.8 copy-done.3
  188.4 1.4 fusion.37
  189.8 223.7 %reduce-scatter.7.cloned.1.call-done = f32[32,2048]{1,0:T(8,128)} async-done(((f32[1024,2048]{1,0:T(8,128)}), f32[32,2048]{1,0:T(8,128)}) %reduce-scatter.7.cloned.1.call-update) | async-done | bytes 262160
  413.5 0.9 slice.55
  414.7 3.5 gather_fusion.3
  418.1 9.3 %fusion.11 = f32[32,512,128]{2,0,1:T(8,128)S(1)} fusion(bf16[512,128,128]{2,1,0:T(8,128)(2,1)} %param.19, bf16[512,32,128]{2,1,0:T(8,128)(2,1)} %gather_fusion.3), kind=kOutput, calls=%fused_computation.16 | convolution fusion | flops 536870912 | bytes 29360128 | tf_op jit(solution)/shard_map/fki,kij->fkj/dot_general | solution.py:83
  427.5 9.6 %fusion = f32[48,32,128]{2,0,1:T(8,128)S(1)} fusion(f32[32,512,128]{2,0,1:T(8,128)S(1)} %fusion.11, f32[512]{0:T(512)S(1)} %fusion.30, s32[512]{0:T(512)S(1)} %copy-done.7), kind=kOutput, calls=%fused_computation.7 | convolution fusion | flops 1208008704 | bytes 9179136 | tf_op jit(solution)/shard_map/fkj,kt->ftj/dot_general | solution.py:84
  438.0 4.3 all-to-all-start.1
  443.3 1.4 fusion.36
  444.7 15.9 %psum.23 = f32[32]{0:T(128)} all-reduce(f32[32]{0:T(128)S(1)} %get-tuple-element.54), channel_id=1, replica_groups=mesh['dom'=8,'feat'=32] {'dom'}, use_global_device_ids=true, to_apply=%region_8.9 | all-reduce | flops 32 | bytes 256 | tf_op jit(solution)/shard_map/psum | solution.py:71
  461.9 7.0 %scatter_fusion = f32[32,4096]{0,1:T(8,128)S(1)} fusion(f32[32,4096]{0,1:T(8,128)S(1)} %copy.99, s32[1024]{0:T(1024)S(1)} %get-tuple-element.59, f32[1024,32]{1,0:T(8,128)S(1)} %copy.90), kind=kCustom, calls=%fused_computation.4 | custom fusion | flops 32768 | bytes 397312 | tf_op jit(solution)/shard_map/scatter-add | solution.py:95
  469.0 9.9 %reduce-scatter.9.cloned.1.call-done = bf16[128,32]{1,0:T(8,128)(2,1)} async-done(((bf16[1024,32]{1,0:T(8,128)(2,1)}), bf16[128,32]{1,0:T(8,128)(2,1)}) %reduce-scatter.9.cloned.1.call-update) | async-done | bytes 8208
  479.8 2.0 scatter_fusion.1
  482.6 1.4 copy.92
  484.0 61.6 %all-reduce.3.cloned.1.call-done = (f32[32,1024]{1,0:T(8,128)}, f32[32,1024]{1,0:T(8,128)}) async-done(((f32[32,1024]{1,0:T(8,128)}, f32[32,1024]{1,0:T(8,128)}), (f32[32,1024]{1,0:T(8,128)}, f32[32,1024]{1,0:T(8,128)})) %all-reduce.3.cloned.1.call-update) | async-done | bytes 262160 | tf_op jit(solution)/shard_map/psum | solution.py:71
  545.6 1.6 copy.132
  547.2 1.6 copy.133
  (67 shorter events, 13.5 us)
Async XLA Ops:
  7.2 162.0 %copy-start = (bf16[32,1024]{1,0:T(8,128)(2,1)S(1)}, bf16[32,1024]{1,0:T(8,128)(2,1)}, u32[]{:S(2)}) copy-start(bf16[32,1024]{1,0:T(8,128)(2,1)} %param.21) | copy-start | bytes 196612
  7.2 83.7 %all-gather.3.cloned.1.call-start = ((), (), s32[]{:S(2)}) async-start(), calls=%async_computation.4 | async-start | bytes 2162688 | tf_op jit(solution)/shard_map/all_gather | solution.py:55
  15.5 21.8 %all-to-all-start = ((bf16[32,8,128]{2,0,1:T(8,128)(2,1)}), bf16[32,8,128]{2,0,1:T(8,128)(2,1)S(1)}, u32[]{:S(2)}, u32[]{:S(2)}) async-start(bf16[32,8,128]{2,0,1:T(8,128)(2,1)} %broadcast_select_fusion), calls=%async_computation | async-start | bytes 131072 | tf_op jit(solution)/shard_map/all_to_all | solution.py:37
  20.0 149.2 %all-gather.5.cloned.1.call-start = ((), (), s32[]{:S(2)}) async-start(), calls=%async_computation.5 | async-start | bytes 2162688 | tf_op jit(solution)/shard_map/all_gather | solution.py:56
  41.8 13.0 %copy-start.6 = (s32[512]{0:T(512)S(1)}, s32[512]{0:T(512)}, u32[]{:S(2)}) copy-start(s32[512]{0:T(512)} %param.16) | copy-start | bytes 6148
  54.8 36.1 %copy-start.4 = (bf16[32,1024]{1,0:T(8,128)(2,1)S(1)}, bf16[32,1024]{1,0:T(8,128)(2,1)}, u32[]{:S(2)}) copy-start(bf16[32,1024]{1,0:T(8,128)(2,1)} %param.20) | copy-start | bytes 196612
  54.8 114.4 %copy-start.5 = (bf16[32,1024]{1,0:T(8,128)(2,1)S(1)}, bf16[32,1024]{1,0:T(8,128)(2,1)}, u32[]{:S(2)}) copy-start(bf16[32,1024]{1,0:T(8,128)(2,1)} %param.23) | copy-start | bytes 196612
  54.8 114.4 %copy-start.8 = (f32[32]{0:T(128)S(1)}, f32[32]{0:T(128)}, u32[]{:S(2)}) copy-start(f32[32]{0:T(128)} %param.22) | copy-start | bytes 388
  64.1 349.3 %reduce-scatter.7.cloned.1.call-start = ((), (), s32[]{:S(2)}) async-start(), calls=%async_computation.6 | async-start | bytes 8650752
  186.8 1.6 copy-start.3
  418.1 9.3 %copy-start.7 = (s32[512]{0:T(512)S(1)}, s32[512]{0:T(512)}, u32[]{:S(2)}) copy-start(s32[512]{0:T(512)} %param.17) | copy-start | bytes 6148
  427.5 15.8 %copy-start.2 = (bf16[1024,1024]{1,0:T(8,128)(2,1)S(1)}, bf16[1024,1024]{1,0:T(8,128)(2,1)}, u32[]{:S(2)}) copy-start(bf16[1024,1024]{1,0:T(8,128)(2,1)} %all-gather.3.cloned.1.call-done) | copy-start | bytes 6291460
  437.1 23.7 %slice-start = ((f32[32,2048]{1,0:T(8,128)}), f32[32,1024]{1,0:T(8,128)S(1)}, s32[]{:S(2)}) async-start(f32[32,2048]{1,0:T(8,128)} %reduce-scatter.7.cloned.1.call-done), calls=%async_computation.9 | async-start | bytes 262144 | tf_op jit(solution)/shard_map/slice | solution.py:80
  438.0 23.7 %all-to-all-start.1 = ((bf16[32,8,128]{2,0,1:T(8,128)(2,1)}), bf16[32,8,128]{2,0,1:T(8,128)(2,1)S(1)}, u32[]{:S(2)}, u32[]{:S(2)}) async-start(bf16[32,8,128]{2,0,1:T(8,128)(2,1)} %bitcast.91), calls=%async_computation.1 | async-start | bytes 131072 | tf_op jit(solution)/shard_map/all_to_all | solution.py:88
  442.3 36.5 %reduce-scatter.9.cloned.1.call-start = ((), (), s32[]{:S(2)}) async-start(), calls=%async_computation.7 | async-start | bytes 294912
  443.2 102.4 %all-reduce.3.cloned.1.call-start = ((), (), s32[]{:S(2)}) async-start(), calls=%async_computation.8 | async-start | bytes 524288 | tf_op jit(solution)/shard_map/psum | solution.py:71
  461.1 87.7 %copy-start.1 = (bf16[32,1024]{1,0:T(8,128)(2,1)S(1)}, bf16[32,1024]{1,0:T(8,128)(2,1)}, u32[]{:S(2)}) copy-start(bf16[32,1024]{1,0:T(8,128)(2,1)} %param.21) | copy-start | bytes 196612
Sparse Core Ops, SparseCore 0:
  11.2 79.6 all-gather.2
  94.1 75.1 all-gather.4
  186.9 226.4 reduce-scatter.6
  446.1 32.6 reduce-scatter.8
  481.6 63.9 all-reduce.2
where the time goes:
time: 556 us; the launch traced here: 555 us
  waiting for transfers between devices  398 us (72%)
  matrix products  49.6 us (9%)
  local copies, waits for them, and re-layouts  34.4 us (6%)
  blocking collectives  29.5 us (5%)
  other arithmetic  19.8 us (4%)
  between operations  14.7 us (3%)
  starting transfers between devices  9.13 us (2%)
    unnamed x7, waiting for transfers between devices  234 us
    all_gather x1, waiting for transfers between devices, body(): lax.all_gather(aggregate, 'feat', axis=0, tiled=True)  76.2 us
    psum x1, waiting for transfers between devices, body(): lax.psum((local_self, local_neigh, local_bias), 'dom')  61.6 us
    all_gather x1, waiting for transfers between devices, body(): lax.all_gather(dst_feats, 'feat', axis=0, tiled=True)  26.6 us
    unnamed x31, local copies, waits for them, and re-layouts  19.8 us
    psum x1, blocking collectives, body(): lax.psum((local_self, local_neigh, local_bias), 'dom')  15.9 us
    all_gather x1, blocking collectives, body(): lax.all_gather(jnp.take(node_feats, hub_rows, axis=1), 'dom', axis=1, til...  13.7 us
    dot_general x1, matrix products, body(): jnp.einsum('fkj,kij->fki', picked, tile_vals, preferred_element_type=jnp....  13 us
  transfers between devices with their start and end apart: 7, of which 5 were waited for; matrix products, arithmetic and copies ran while one was open for 10% of the time, Pallas kernels for 0%

commit v1 on v0

--- a/solution.py
+++ b/solution.py
@@ -53,7 +53,9 @@
     dst_feats = node_feats[:, :dst_rows]
     whole_self, whole_agg = (
         lax.all_gather(dst_feats, "feat", axis=0, tiled=True),
-        lax.all_gather(aggregate, "feat", axis=0, tiled=True),
+        jnp.concatenate(
+            lax.all_to_all(jnp.stack([aggregate] * lax.axis_size("feat")), "feat", 0, 0), axis=0
+        ),
     )
     pre_act = (
         jnp.dot(w_self, whole_self, preferred_element_type=jnp.float32)

time: 556 us -> 515 us (0.926)
  waiting for transfers between devices: 398 us -> 347 us
  starting transfers between devices: 9.13 us -> 20.5 us
    all_gather x1 -> x0, waiting for transfers between devices: 76.2 us -> none  [body(): lax.all_gather(aggregate, 'feat', axis=0, tiled=True)]
    all_to_all x0 -> x1, waiting for transfers between devices: none -> 33.4 us  [body(): lax.all_to_all(jnp.stack([aggregate] * lax.axis_size('feat')), 'feat', 0, 0)]
    all_to_all x0 -> x1, starting transfers between devices: none -> 11.6 us  [body(): lax.all_to_all(jnp.stack([aggregate] * lax.axis_size('feat')), 'feat', 0, 0)]
    all_gather x1, waiting for transfers between devices: 26.6 us -> 18.6 us  [body(): lax.all_gather(dst_feats, 'feat', axis=0, tiled=True)]
    unnamed x31 -> x29, local copies, waits for them, and re-layouts: 19.8 us -> 18.3 us
    unnamed x7 -> x6, waiting for transfers between devices: 234 us -> 233 us
  transfers between devices with their start and end apart: 7 -> 7, of which waited for: 5 -> 5; matrix products, arithmetic and copies ran while one was open for 10% -> 11% of each run, Pallas kernels for 0% -> 0%
where the time goes in v1:
time: 515 us; the launch traced here: 514 us
  waiting for transfers between devices  347 us (67%)
  matrix products  48.3 us (9%)
  local copies, waits for them, and re-layouts  34.5 us (7%)
  blocking collectives  29.5 us (6%)
  starting transfers between devices  20.5 us (4%)
  other arithmetic  19.8 us (4%)
  between operations  14.7 us (3%)
    unnamed x6, waiting for transfers between devices  233 us
    psum x1, waiting for transfers between devices, body(): lax.psum((local_self, local_neigh, local_bias), 'dom')  61.7 us
    all_to_all x1, waiting for transfers between devices, body(): lax.all_to_all(jnp.stack([aggregate] * lax.axis_size('feat')), 'feat', 0, 0)  33.4 us
    all_gather x1, waiting for transfers between devices, body(): lax.all_gather(dst_feats, 'feat', axis=0, tiled=True)  18.6 us
    unnamed x29, local copies, waits for them, and re-layouts  18.3 us
    psum x1, blocking collectives, body(): lax.psum((local_self, local_neigh, local_bias), 'dom')  15.9 us
    all_gather x1, blocking collectives, body(): lax.all_gather(jnp.take(node_feats, hub_rows, axis=1), 'dom', axis=1, til...  13.7 us
    dot_general x1, matrix products, body(): jnp.einsum('fkj,kij->fki', picked, tile_vals, preferred_element_type=jnp....  13 us
  transfers between devices with their start and end apart: 7, of which 5 were waited for; matrix products, arithmetic and copies ran while one was open for 11% of the time, Pallas kernels for 0%

profile of v1, /device:TPU:2, one launch (start us, length us, event | category | flops | bytes accessed | tf_op | source)
XLA Modules:
  0.0 514.0 jit_solution(10461168480133183761)
XLA Ops:
  7.2 1.5 slice.40
  10.1 1.4 copy.77
  11.5 3.2 gather_fusion
  15.5 4.5 all-to-all-start
  23.5 13.7 %all_gather.7 = bf16[32,1024]{0,1:T(8,128)(2,1)S(1)} all-gather(bf16[32,128]{0,1:T(8,128)(2,1)S(1)} %select_bitcast_fusion), channel_id=1, replica_groups=mesh['dom'=8,'feat'=32] {'dom'}, dimensions={1}, use_global_device_ids=true | all-gather | bytes 73728 | tf_op jit(solution)/shard_map/all_gather | solution.py:38
  37.3 1.0 copy_bitcast_fusion.1
  38.4 3.5 gather_fusion.2
  41.8 13.0 %fusion.8 = f32[32,512,128]{2,0,1:T(8,128)S(1)} fusion(bf16[512,128,128]{2,1,0:T(8,128)(2,1)} %param.19, bf16[512,32,128]{2,1,0:T(8,128)(2,1)} %gather_fusion.2), kind=kOutput, calls=%fused_computation.15 | convolution fusion | flops 536870912 | bytes 29360128 | tf_op jit(solution)/shard_map/fkj,kij->fki/dot_general | solution.py:50
  54.8 8.6 %fusion.16 = bf16[8,32,128]{2,0,1:T(8,128)(2,1)S(1)} fusion(f32[32,512,128]{2,0,1:T(8,128)S(1)} %fusion.8, f32[512]{0:T(512)S(1)} %fusion.30, s32[512]{0:T(512)S(1)} %copy-done.5), kind=kOutput, calls=%fused_computation.22 | convolution fusion | flops 201367552 | bytes 8458240 | tf_op jit(solution)/shard_map/fki,ku->fui/dot_general | solution.py:51
  63.5 1.6 stack.2
  65.1 11.6 %all-to-all-start.1 = ((bf16[32,32,1024]{2,1,0:T(8,128)(2,1)}), bf16[32,32,1024]{2,1,0:T(8,128)(2,1)S(1)}, u32[]{:S(2)}, u32[]{:S(2)}) async-start(bf16[32,32,1024]{2,1,0:T(8,128)(2,1)} %stack.2), calls=%async_computation.1 | async-start | bytes 4194304 | tf_op jit(solution)/shard_map/all_to_all | solution.py:57
  76.7 18.6 %all-gather.2.cloned.1.call-done = bf16[1024,1024]{1,0:T(8,128)(2,1)} async-done(((bf16[32,1024]{1,0:T(8,128)(2,1)}), bf16[1024,1024]{1,0:T(8,128)(2,1)}) %all-gather.2.cloned.1.call-update) | async-done | bytes 2097168 | tf_op jit(solution)/shard_map/all_gather | solution.py:55
  95.3 2.1 fusion.35
  97.4 33.4 %all-to-all-done.1 = bf16[32,32,1024]{2,1,0:T(8,128)(2,1)S(1)} async-done(((bf16[32,32,1024]{2,1,0:T(8,128)(2,1)}), bf16[32,32,1024]{2,1,0:T(8,128)(2,1)S(1)}, u32[]{:S(2)}, u32[]{:S(2)}) %all-to-all-start.1) | async-done | bytes 2097184 | tf_op jit(solution)/shard_map/all_to_all | solution.py:57
  130.8 1.2 convert_reduce_fusion
  133.5 4.1 pad_maximum_fusion
  137.6 9.2 %copy.95 = f32[1024,2048]{1,0:T(8,128)} copy(f32[1024,2048]{0,1:T(8,128)} %pad_maximum_fusion) | data formatting | bytes 16777216
  147.5 1.4 fusion.37
  148.9 222.8 %reduce-scatter.7.cloned.1.call-done = f32[32,2048]{1,0:T(8,128)} async-done(((f32[1024,2048]{1,0:T(8,128)}), f32[32,2048]{1,0:T(8,128)}) %reduce-scatter.7.cloned.1.call-update) | async-done | bytes 262160
  372.8 3.5 gather_fusion.3
  376.3 9.5 %fusion.11 = f32[32,512,128]{2,0,1:T(8,128)S(1)} fusion(bf16[512,128,128]{2,1,0:T(8,128)(2,1)} %param.19, bf16[512,32,128]{2,1,0:T(8,128)(2,1)} %gather_fusion.3), kind=kOutput, calls=%fused_computation.16 | convolution fusion | flops 536870912 | bytes 29360128 | tf_op jit(solution)/shard_map/fki,kij->fkj/dot_general | solution.py:85
  385.9 9.6 %fusion = f32[48,32,128]{2,0,1:T(8,128)S(1)} fusion(f32[32,512,128]{2,0,1:T(8,128)S(1)} %fusion.11, f32[512]{0:T(512)S(1)} %fusion.30, s32[512]{0:T(512)S(1)} %copy-done.6), kind=kOutput, calls=%fused_computation.7 | convolution fusion | flops 1208008704 | bytes 9179136 | tf_op jit(solution)/shard_map/fkj,kt->ftj/dot_general | solution.py:86
  396.4 4.3 all-to-all-start.2
  401.6 1.4 fusion.36
  403.1 15.9 %psum.23 = f32[32]{0:T(128)} all-reduce(f32[32]{0:T(128)S(1)} %get-tuple-element.54), channel_id=1, replica_groups=mesh['dom'=8,'feat'=32] {'dom'}, use_global_device_ids=true, to_apply=%region_8.9 | all-reduce | flops 32 | bytes 256 | tf_op jit(solution)/shard_map/psum | solution.py:73
  420.3 7.1 %scatter_fusion = f32[32,4096]{0,1:T(8,128)S(1)} fusion(f32[32,4096]{0,1:T(8,128)S(1)} %copy.99, s32[1024]{0:T(1024)S(1)} %get-tuple-element.59, f32[1024,32]{1,0:T(8,128)S(1)} %copy.90), kind=kCustom, calls=%fused_computation.4 | custom fusion | flops 32768 | bytes 397312 | tf_op jit(solution)/shard_map/scatter-add | solution.py:97
  427.3 10.1 %reduce-scatter.9.cloned.1.call-done = bf16[128,32]{1,0:T(8,128)(2,1)} async-done(((bf16[1024,32]{1,0:T(8,128)(2,1)}), bf16[128,32]{1,0:T(8,128)(2,1)}) %reduce-scatter.9.cloned.1.call-update) | async-done | bytes 8208
  438.4 2.0 scatter_fusion.1
  441.2 1.4 copy.92
  442.6 61.7 %all-reduce.3.cloned.1.call-done = (f32[32,1024]{1,0:T(8,128)}, f32[32,1024]{1,0:T(8,128)}) async-done(((f32[32,1024]{1,0:T(8,128)}, f32[32,1024]{1,0:T(8,128)}), (f32[32,1024]{1,0:T(8,128)}, f32[32,1024]{1,0:T(8,128)})) %all-reduce.3.cloned.1.call-update) | async-done | bytes 262160 | tf_op jit(solution)/shard_map/psum | solution.py:73
  504.3 1.6 copy.132
  505.9 1.6 copy.133
  (65 shorter events, 13.5 us)
Async XLA Ops:
  7.2 123.6 %copy-start = (bf16[32,1024]{1,0:T(8,128)(2,1)S(1)}, bf16[32,1024]{1,0:T(8,128)(2,1)}, u32[]{:S(2)}) copy-start(bf16[32,1024]{1,0:T(8,128)(2,1)} %param.21) | copy-start | bytes 196612
  7.2 88.2 %all-gather.2.cloned.1.call-start = ((), (), s32[]{:S(2)}) async-start(), calls=%async_computation.5 | async-start | bytes 2162688 | tf_op jit(solution)/shard_map/all_gather | solution.py:55
  15.5 21.8 %all-to-all-start = ((bf16[32,8,128]{2,0,1:T(8,128)(2,1)}), bf16[32,8,128]{2,0,1:T(8,128)(2,1)S(1)}, u32[]{:S(2)}, u32[]{:S(2)}) async-start(bf16[32,8,128]{2,0,1:T(8,128)(2,1)} %broadcast_select_fusion), calls=%async_computation | async-start | bytes 131072 | tf_op jit(solution)/shard_map/all_to_all | solution.py:37
  41.8 13.0 %copy-start.5 = (s32[512]{0:T(512)S(1)}, s32[512]{0:T(512)}, u32[]{:S(2)}) copy-start(s32[512]{0:T(512)} %param.16) | copy-start | bytes 6148
  63.4 31.9 %copy-start.3 = (bf16[32,1024]{1,0:T(8,128)(2,1)S(1)}, bf16[32,1024]{1,0:T(8,128)(2,1)}, u32[]{:S(2)}) copy-start(bf16[32,1024]{1,0:T(8,128)(2,1)} %param.20) | copy-start | bytes 196612
  63.4 67.3 %copy-start.4 = (bf16[32,1024]{1,0:T(8,128)(2,1)S(1)}, bf16[32,1024]{1,0:T(8,128)(2,1)}, u32[]{:S(2)}) copy-start(bf16[32,1024]{1,0:T(8,128)(2,1)} %param.23) | copy-start | bytes 196612
  63.4 67.3 %copy-start.7 = (f32[32]{0:T(128)S(1)}, f32[32]{0:T(128)}, u32[]{:S(2)}) copy-start(f32[32]{0:T(128)} %param.22) | copy-start | bytes 388
  65.1 65.7 %all-to-all-start.1 = ((bf16[32,32,1024]{2,1,0:T(8,128)(2,1)}), bf16[32,32,1024]{2,1,0:T(8,128)(2,1)S(1)}, u32[]{:S(2)}, u32[]{:S(2)}) async-start(bf16[32,32,1024]{2,1,0:T(8,128)(2,1)} %stack.2), calls=%async_computation.1 | async-start | bytes 4194304 | tf_op jit(solution)/shard_map/all_to_all | solution.py:57
  76.7 294.9 %reduce-scatter.7.cloned.1.call-start = ((), (), s32[]{:S(2)}) async-start(), calls=%async_computation.6 | async-start | bytes 8650752
  376.3 9.5 %copy-start.6 = (s32[512]{0:T(512)S(1)}, s32[512]{0:T(512)}, u32[]{:S(2)}) copy-start(s32[512]{0:T(512)} %param.17) | copy-start | bytes 6148
  385.8 15.8 %copy-start.2 = (bf16[1024,1024]{1,0:T(8,128)(2,1)S(1)}, bf16[1024,1024]{1,0:T(8,128)(2,1)}, u32[]{:S(2)}) copy-start(bf16[1024,1024]{1,0:T(8,128)(2,1)} %all-gather.2.cloned.1.call-done) | copy-start | bytes 6291460
  395.5 23.7 %slice-start = ((f32[32,2048]{1,0:T(8,128)}), f32[32,1024]{1,0:T(8,128)S(1)}, s32[]{:S(2)}) async-start(f32[32,2048]{1,0:T(8,128)} %reduce-scatter.7.cloned.1.call-done), calls=%async_computation.9 | async-start | bytes 262144 | tf_op jit(solution)/shard_map/slice | solution.py:82
  396.4 23.6 %all-to-all-start.2 = ((bf16[32,8,128]{2,0,1:T(8,128)(2,1)}), bf16[32,8,128]{2,0,1:T(8,128)(2,1)S(1)}, u32[]{:S(2)}, u32[]{:S(2)}) async-start(bf16[32,8,128]{2,0,1:T(8,128)(2,1)} %bitcast.92), calls=%async_computation.2 | async-start | bytes 131072 | tf_op jit(solution)/shard_map/all_to_all | solution.py:90
  400.7 36.8 %reduce-scatter.9.cloned.1.call-start = ((), (), s32[]{:S(2)}) async-start(), calls=%async_computation.7 | async-start | bytes 294912
  401.6 102.7 %all-reduce.3.cloned.1.call-start = ((), (), s32[]{:S(2)}) async-start(), calls=%async_computation.8 | async-start | bytes 524288 | tf_op jit(solution)/shard_map/psum | solution.py:73
  419.4 88.0 %copy-start.1 = (bf16[32,1024]{1,0:T(8,128)(2,1)S(1)}, bf16[32,1024]{1,0:T(8,128)(2,1)}, u32[]{:S(2)}) copy-start(bf16[32,1024]{1,0:T(8,128)(2,1)} %param.21) | copy-start | bytes 196612
Sparse Core Ops, SparseCore 0:
  11.2 84.1 all-gather.1
  146.9 224.6 reduce-scatter.6
  404.7 32.6 reduce-scatter.8
  440.3 63.9 all-reduce.2
